TPU v7x, 32 devices: a whole 2x2x4 slice. The times are simulated.
32 devices in a mesh: dom: 16 (over z, y, x), row: 2 (over core).
Axes of the slice: x: 2, y: 2, z: 4, core: 2. Of those that a mesh axis runs over, the one named last changes fastest.
Arguments:
- features: float32 [4096, 128], P(('dom', 'row')), may hold values from -6 to 6
- history: float32 [4096, 1024], P(('dom', 'row')), may hold values from -3 to 3
- tiles: float32 [32, 4, 128, 128], P(('dom', 'row')), may hold values from -0.25 to 0.25
- tile_cols: int32 [32, 4], P(('dom', 'row')), may hold values from 0 to 1
- cross_weight: float32 [4096, 128], P(('dom', 'row')), may hold values from -0.75 to 0.75
- send_rows: int32 [32, 16, 8], P(('dom', 'row')), may hold values from 0 to 127
- send_count: int32 [32, 16], P(('dom', 'row')), may hold values from 0 to 8, as said below
- cotangent: float32 [4096, 172], P(('dom', 'row')), may hold values from -0.0234375 to 0.0234375
- w_one: float32 [128, 1024], replicated, may hold values from -0.5 to 0.5
- w_two: float32 [1024, 172], replicated, may hold values from -0.1875 to 0.1875
Outputs:
- logits: float32 [4096, 172], P(('dom', 'row'))
- grad_w1: float32 [128, 1024], replicated
- grad_w2: float32 [1024, 172], replicated
Inputs may be any that keep to these rules, and one draw needn't show every extreme that they name: send_count is 0 toward the sender's own partition; in every draw some partition receives 8 live rows from every device of every other partition.
All inputs are finite; a program needn't handle non-finite values.
Results may differ from a plain program's by a relative error of at most 0.0003.
Values sent between devices are 32-bit elements; how exact they have to be, the bound alone decides.
A program may use at most 64 MiB of HBM per device.

v0:
```python
import jax
import jax.numpy as jnp
from jax import lax
from jax.sharding import PartitionSpec as P

HIGH = lax.Precision.HIGHEST


def gate_act(values):
    sigma = jax.nn.sigmoid(values)
    return (values * sigma, sigma * (1.0 + values * (1.0 - sigma)))


def matmul(left, right):
    return jnp.dot(left, right, precision=HIGH, preferred_element_type=jnp.float32)


def on_device(
    features,
    history,
    tiles,
    tile_cols,
    cross_weight,
    send_rows,
    send_count,
    cotangent,
    w_one,
    w_two,
):
    rows_here = features.shape[0]
    blocks_here = tiles.shape[0]
    parts_count = send_rows.shape[1]
    slot_count = send_rows.shape[2]
    width_in = features.shape[1]
    width_hidden = history.shape[1]
    width_out = w_two.shape[1]
    lane_index = jnp.arange(128, dtype=jnp.int32)
    targets = tile_cols[:, :, None] * 128 + lane_index[None, None, :]
    live_mask = (jnp.arange(slot_count, dtype=jnp.int32)[None, :] < send_count[0][:, None]).astype(
        jnp.float32
    )
    pick_rows = send_rows[0]
    feat_out = jnp.take(features, pick_rows, axis=0) * live_mask[:, :, None]
    hist_out = jnp.take(history, pick_rows, axis=0) * live_mask[:, :, None]
    got_feat, got_hist = (
        lax.all_to_all(feat_out, "dom", split_axis=0, concat_axis=0, tiled=True),
        lax.all_to_all(hist_out, "dom", split_axis=0, concat_axis=0, tiled=True),
    )
    cross_feat = matmul(cross_weight, got_feat.reshape(parts_count * slot_count, width_in))
    cross_hist = matmul(cross_weight, got_hist.reshape(parts_count * slot_count, width_hidden))
    cross_logits = matmul(cross_hist, w_two)

    def add_panel(panel):
        row_count = panel.shape[0]
        inside = (targets >= 0) & (targets < row_count)
        picked = jnp.take(panel, jnp.clip(targets, 0, row_count - 1), axis=0)
        picked = picked * inside[..., None].astype(panel.dtype)
        return jnp.einsum("bkij,bkjw->biw", tiles, picked, precision=HIGH)

    local_feat = add_panel(lax.all_gather(features, "row", axis=0, tiled=True))
    layer_in = local_feat.reshape(rows_here, width_in) + cross_feat
    pre_act = matmul(layer_in, w_one)
    hidden, slope_gate = gate_act(pre_act)
    projected = matmul(hidden, w_two)
    local_out = add_panel(lax.all_gather(projected, "row", axis=0, tiled=True))
    logits = local_out.reshape(rows_here, width_out) + cross_logits
    blocked_grads = cotangent.reshape(blocks_here, 128, width_out)
    contrib = jnp.einsum("bkij,biw->bkjw", tiles, blocked_grads, precision=HIGH)
    block_ids = jnp.arange(lax.axis_size("row") * rows_here // 128, dtype=jnp.int32)
    hot = (tile_cols[:, :, None] == block_ids[None, None, :]).astype(jnp.float32)
    summed = jnp.einsum("bkc,bkjw->cjw", hot, contrib, precision=HIGH)
    back_grad = lax.psum_scatter(
        summed.reshape(lax.axis_size("row") * rows_here // 128 * 128, width_out),
        "row",
        scatter_dimension=0,
        tiled=True,
    )
    grad_two = matmul(hidden.T, back_grad)
    grad_two = grad_two + matmul(cross_hist.T, cotangent)
    grad_pre = matmul(back_grad, w_two.T) * slope_gate
    grad_one = matmul(layer_in.T, grad_pre)
    grad_one, grad_two = lax.psum((grad_one, grad_two), ("dom", "row"))
    return (logits, grad_one, grad_two)


def solution(mesh):
    placed = (
        P(("dom", "row"), None),
        P(("dom", "row"), None),
        P(("dom", "row"), None, None, None),
        P(("dom", "row"), None),
        P(("dom", "row"), None),
        P(("dom", "row"), None, None),
        P(("dom", "row"), None),
        P(("dom", "row"), None),
        P(),
        P(),
    )
    return jax.shard_map(
        on_device,
        mesh=mesh,
        in_specs=placed,
        out_specs=(P(("dom", "row"), None), P(), P()),
        check_vma=False,
    )
```

profile of v0, /device:TPU:1, one launch (start us, length us, event | category | flops | bytes accessed | tf_op | source)
XLA Modules:
  0.0 193.2 jit_solution(11159465152291520125)
XLA Ops:
  7.2 0.0 copy-start
  7.2 0.0 copy-start.10
  7.2 0.8 compare_and_fusion
  8.0 0.0 copy-done.10
  8.0 0.1 copy.20
  8.1 0.1 copy.21
  8.1 0.1 reshape.276
  8.2 0.0 copy-start.12
  8.2 0.6 copy-done.12
  8.9 0.1 fusion.26
  9.0 1.5 gather_fusion.1
  10.5 0.7 fusion.25
  11.2 7.4 %all-to-all-start = ((f32[16,8,128]{2,1,0:T(8,128)}), f32[16,8,128]{2,1,0:T(8,128)S(1)}, u32[]{:S(2)}, u32[]{:S(2)}) async-start(f32[16,8,128]{2,1,0:T(8,128)} %fusion.25), calls=%async_computation | async-start | bytes 131072 | tf_op jit(solution)/shard_map/all_to_all | solution.py:46
  18.6 0.0 reduce-scatter.2.cloned.1.call-start
  18.7 0.0 copy-done.6
  18.7 0.0 copy-done.3
  18.7 0.5 fusion.7
  19.2 0.0 copy-start.11
  19.2 0.6 copy-done.11
  19.8 0.5 convolution_bitcast_fusion
  20.3 0.1 pad.4
  20.4 0.7 copy.26
  21.1 0.0 reduce-scatter.2.cloned.1.call-update
  21.1 0.1 fusion.27
  21.2 0.1 compare_and_fusion.1
  21.3 0.6 copy-done.2
  21.9 2.5 %all_gather.6 = f32[256,128]{1,0:T(8,128)S(1)} all-gather(f32[128,128]{1,0:T(8,128)S(1)} %copy-done.2), channel_id=1, replica_groups=mesh['dom'=16,'row'=2] {'row'}, dimensions={0}, use_global_device_ids=true | all-gather | bytes 196608 | tf_op jit(solution)/shard_map/all_gather | solution.py:60
  24.4 1.0 gather_fusion
  25.5 0.0 copy-start.1
  25.5 0.1 copy.19
  25.6 0.9 copy-done.1
  26.5 0.8 gather_fusion.3
  27.3 0.9 fusion.2
  28.2 0.4 convolution_bitcast_fusion.2
  28.6 0.0 copy-start.8
  28.6 0.0 copy-start.5
  28.7 0.0 all-to-all-done
  28.7 6.8 %all-to-all-start.1 = ((f32[16,8,1024]{2,1,0:T(8,128)}), f32[16,8,1024]{2,1,0:T(8,128)S(1)}, u32[]{:S(2)}, u32[]{:S(2)}) async-start(f32[16,8,1024]{2,1,0:T(8,128)} %fusion.2), calls=%async_computation.1 | async-start | bytes 1048576 | tf_op jit(solution)/shard_map/all_to_all | solution.py:47
  35.4 0.0 all-reduce.3.cloned.1.call-start
  35.5 0.0 copy-done.8
  35.5 0.3 convolution_add_fusion.2
  35.8 0.0 copy-done.5
  35.8 0.6 fusion.40
  36.4 0.0 reduce-scatter.2.cloned.1.call-done
  36.5 0.0 copy-done
  36.5 1.6 convolution_multiply_fusion
  38.1 1.4 fusion.41
  39.5 0.0 copy-done.13
  39.5 0.9 fusion.20
  40.4 0.0 copy-start.7
  40.4 7.7 %all-to-all-done.1 = f32[16,8,1024]{2,1,0:T(8,128)S(1)} async-done(((f32[16,8,1024]{2,1,0:T(8,128)}), f32[16,8,1024]{2,1,0:T(8,128)S(1)}, u32[]{:S(2)}, u32[]{:S(2)}) %all-to-all-start.1) | async-done | bytes 524320 | tf_op jit(solution)/shard_map/all_to_all | solution.py:47
  48.1 1.0 fusion
  49.1 1.6 convolution_add_fusion
  50.7 0.0 all-reduce.3.cloned.1.call-update
  50.8 0.8 fusion.22
  51.6 5.0 %all_gather.7 = f32[256,172]{0,1:T(8,128)S(1)} all-gather(f32[128,172]{0,1:T(8,128)S(1)} %fusion.22), channel_id=1, replica_groups=mesh['dom'=16,'row'=2] {'row'}, dimensions={0}, use_global_device_ids=true | all-gather | bytes 264192 | tf_op jit(solution)/shard_map/all_gather | solution.py:65
  56.6 0.1 copy.22
  56.7 1.6 gather_fusion.2
  58.3 0.2 copy.23
  58.5 0.5 convolution_bitcast_fusion.1
  59.0 1.4 convolution_add_fusion.1
  60.3 123.2 %all-reduce.3.cloned.1.call-done = (f32[128,1024]{1,0:T(8,128)}, f32[1024,172]{0,1:T(8,128)}) async-done(((f32[128,1024]{1,0:T(8,128)}, f32[1024,172]{0,1:T(8,128)}), (f32[128,1024]{1,0:T(8,128)}, f32[1024,172]{0,1:T(8,128)})) %all-reduce.3.cloned.1.call-update) | async-done | bytes 1228816 | tf_op jit(solution)/shard_map/psum | solution.py:82
  183.5 2.0 %copy.31 = f32[128,1024]{1,0:T(8,128)} copy(f32[128,1024]{1,0:T(8,128)} %get-tuple-element.8) | data formatting | bytes 1048576
  185.5 0.9 copy.32
  (13 shorter events, 0.0 us)
Async XLA Ops:
  7.2 29.3 %copy-start = (f32[1024,172]{0,1:T(8,128)S(1)}, f32[1024,172]{0,1:T(8,128)}, u32[]{:S(2)}) copy-start(f32[1024,172]{0,1:T(8,128)} %param.19) | copy-start | bytes 2113540
  7.2 0.8 copy-start.10
  8.2 0.7 copy-start.12
  9.0 9.7 %copy-start.6 = (f32[128,172]{0,1:T(8,128)S(1)}, f32[128,172]{0,1:T(8,128)}, u32[]{:S(2)}) copy-start(f32[128,172]{0,1:T(8,128)} %param.17) | copy-start | bytes 264196
  10.5 8.2 %copy-start.3 = (f32[1,4,128,128]{3,2,1,0:T(8,128)S(1)}, f32[1,4,128,128]{3,2,1,0:T(8,128)}, u32[]{:S(2)}) copy-start(f32[1,4,128,128]{3,2,1,0:T(8,128)} %param.12) | copy-start | bytes 786436
  11.2 17.4 %all-to-all-start = ((f32[16,8,128]{2,1,0:T(8,128)}), f32[16,8,128]{2,1,0:T(8,128)S(1)}, u32[]{:S(2)}, u32[]{:S(2)}) async-start(f32[16,8,128]{2,1,0:T(8,128)} %fusion.25), calls=%async_computation | async-start | bytes 131072 | tf_op jit(solution)/shard_map/all_to_all | solution.py:46
  18.6 17.8 %reduce-scatter.2.cloned.1.call-start = ((), (), s32[]{:S(2)}) async-start(), calls=%async_computation.3 | async-start | bytes 270336 | tf_op jit(solution)/shard_map/reduce_scatter | solution.py:72
  19.2 0.7 copy-start.11
  21.1 0.8 copy-start.2
  25.5 1.0 copy-start.1
  28.6 6.9 %copy-start.8 = (f32[128,128]{1,0:T(8,128)S(1)}, f32[128,128]{1,0:T(8,128)}, u32[]{:S(2)}) copy-start(f32[128,128]{1,0:T(8,128)} %param.14) | copy-start | bytes 196612
  28.6 7.2 %copy-start.5 = (f32[128,1024]{1,0:T(8,128)S(1)}, f32[128,1024]{1,0:T(8,128)}, u32[]{:S(2)}) copy-start(f32[128,1024]{1,0:T(8,128)} %param.18) | copy-start | bytes 1572868
  28.7 19.4 %all-to-all-start.1 = ((f32[16,8,1024]{2,1,0:T(8,128)}), f32[16,8,1024]{2,1,0:T(8,128)S(1)}, u32[]{:S(2)}, u32[]{:S(2)}) async-start(f32[16,8,1024]{2,1,0:T(8,128)} %fusion.2), calls=%async_computation.1 | async-start | bytes 1048576 | tf_op jit(solution)/shard_map/all_to_all | solution.py:47
  35.4 148.1 %all-reduce.3.cloned.1.call-start = ((), (), s32[]{:S(2)}) async-start(), calls=%async_computation.4 | async-start | bytes 2490368 | tf_op jit(solution)/shard_map/psum | solution.py:82
  38.1 1.4 copy-start.13
  39.5 8.6 %copy-start.9 = (f32[128,128]{1,0:T(8,128)S(1)}, f32[128,128]{1,0:T(8,128)}, u32[]{:S(2)}) copy-start(f32[128,128]{1,0:T(8,128)} %param.14) | copy-start | bytes 196612
  40.4 8.7 %copy-start.7 = (f32[128,172]{0,1:T(8,128)S(1)}, f32[128,172]{0,1:T(8,128)}, u32[]{:S(2)}) copy-start(f32[128,172]{0,1:T(8,128)} %param.17) | copy-start | bytes 264196
  183.5 2.0 %copy-start.4 = (f32[1024,172]{0,1:T(8,128)S(1)}, f32[1024,172]{0,1:T(8,128)}, u32[]{:S(2)}) copy-start(f32[1024,172]{0,1:T(8,128)} %get-tuple-element.9) | copy-start | bytes 2113540
Sparse Core Ops, SparseCore 0:
  22.2 9.5 reduce-scatter.1
  50.9 132.6 all-reduce.2
where the time goes:
time: 194 us; the launch traced here: 193 us
  waiting for transfers between devices  131 us (68%)
  between operations  14.4 us (7%)
  starting transfers between devices  14.3 us (7%)
  local copies, waits for them, and re-layouts  12.1 us (6%)
  matrix products  11.4 us (6%)
  blocking collectives  7.46 us (4%)
  other arithmetic  2.67 us (1%)
    psum x1, waiting for transfers between devices, on_device(): grad_one, grad_two = lax.psum((grad_one, grad_two), ('dom', 'row'))  123 us
    dot_general x9, matrix products, matmul(): jnp.dot(left, right, precision=HIGH, preferred_element_type=jnp.float32)  9.62 us
    all_to_all x1, waiting for transfers between devices, on_device(): lax.all_to_all(hist_out, 'dom', split_axis=0, concat_axis=0, tiled=True)  7.7 us
    all_to_all x1, starting transfers between devices, on_device(): lax.all_to_all(feat_out, 'dom', split_axis=0, concat_axis=0, tiled=True)  7.4 us
    all_to_all x1, starting transfers between devices, on_device(): lax.all_to_all(hist_out, 'dom', split_axis=0, concat_axis=0, tiled=True)  6.77 us
    unnamed x32, local copies, waits for them, and re-layouts  6.46 us
    all_gather x1, blocking collectives, on_device(): local_out = add_panel(lax.all_gather(projected, 'row', axis=0, tiled=True))  4.97 us
  transfers between devices with their start and end apart: 4, of which 2 were waited for; matrix products, arithmetic and copies ran while one was open for 7% of the time, Pallas kernels for 0%

commit v1 on v0

v1 whole, which is shorter than its diff:
```python
import functools
import math

import jax
import jax.numpy as jnp
from jax import lax
from jax.experimental import pallas as pl
from jax.experimental.pallas import tpu as pltpu
from jax.sharding import PartitionSpec as P

MESH = pl.DeviceIdType.MESH
F32 = jnp.float32
BF16 = jnp.bfloat16
NN = (((1,), (0,)), ((), ()))
NT = (((1,), (1,)), ((), ()))


def split(values):
    high = values.astype(BF16)
    return high, (values - high.astype(F32)).astype(BF16)


def dot(left, right, dims=NN):
    one = functools.partial(lax.dot_general, dimension_numbers=dims, preferred_element_type=F32)
    (lh, ll), (rh, rl) = left, right
    return one(lh, rh) + (one(lh, rl) + one(ll, rh))


def pick(chosen, right):
    one = functools.partial(lax.dot_general, dimension_numbers=NN, preferred_element_type=F32)
    return one(chosen, right[0]) + one(chosen, right[1])


def round_up(value, unit):
    return -(-value // unit) * unit


def factors(length):
    inner = 2 ** int(math.log2(math.isqrt(length)))
    return length // inner, inner


def kernel(
    sizes,
    cols_ref, feat_ref, hist_ref, tiles_ref, cw_ref, rows_ref, count_ref, cot_ref, w1_ref, w2_ref,
    logits_ref, g1_ref, g2_ref,
    cotp, w2p, w2h, w2l, adj, fpack, frecv, hpack, hrecv, wpack, wrecv, panel,
    proj, tsend, trecv, hh, hl, slope, grads, rb1, a1, rb2, a2, rb3, full,
    s_feat, r_feat, s_hist, r_hist, s_back, r_back, s_panel, r_panel, s_proj, r_proj, s_tr, r_tr,
    s_row, r_row, s_in, r_in, s_out, r_out, s_gout, r_gout, s_gin, r_gin, s_grow, r_grow,
):
    D, R, O, I, LB = sizes
    NB = w1_ref.shape[1] // 128
    nb = NB // R
    TR = nb * LB
    IP = TR // I
    OP = IP // O
    slots = rows_ref.shape[0]
    NS = D * slots
    C = cot_ref.shape[0]
    C8 = round_up(C, 8)
    CP = cotp.shape[0]
    F = feat_ref.shape[1]
    H = w1_ref.shape[1]
    d = lax.axis_index("dom")
    r = lax.axis_index("row")
    o = d // I
    i = lax.rem(d, I)
    pending = []

    def at(value, unit):
        return pl.multiple_of(value * unit, unit)

    def remote(src, dst, ss, rs, dom, row):
        return pltpu.make_async_remote_copy(
            src_ref=src, dst_ref=dst, send_sem=ss, recv_sem=rs,
            device_id=(dom, row), device_id_type=MESH)

    barrier = pltpu.get_barrier_semaphore()

    def greet(k, carry):
        pl.semaphore_signal(barrier, inc=1, device_id=(lax.rem(d + k, D), r), device_id_type=MESH)
        return carry

    for k in range(1, R):
        pl.semaphore_signal(barrier, inc=1, device_id=(d, lax.rem(r + k, R)), device_id_type=MESH)
    lax.fori_loop(1, D, greet, 0)

    live = lax.broadcasted_iota(jnp.int32, (slots, D), 0) < count_ref[...]
    wanted = jnp.where(live, rows_ref[...], -1).astype(F32).astype(BF16)
    spread = (lax.broadcasted_iota(jnp.int32, (D, NS), 1) // slots
              == lax.broadcasted_iota(jnp.int32, (D, NS), 0)).astype(F32).astype(BF16)
    wide = lax.dot_general(wanted, spread, NN, preferred_element_type=F32)
    own = (lax.rem(lax.broadcasted_iota(jnp.int32, (slots, NS), 1), slots)
           == lax.broadcasted_iota(jnp.int32, (slots, NS), 0))
    row_of = jnp.sum(jnp.where(own, wide, 0.0), axis=0, keepdims=True)
    node = lax.broadcasted_iota(jnp.int32, (128, NS), 0).astype(F32)
    back_f = (node == row_of).astype(F32)
    back_pick = back_f.astype(BF16)
    send_pick = back_f.T.astype(BF16)

    feat = split(feat_ref[...])
    fpack[...] = pick(send_pick, feat)

    pl.semaphore_wait(barrier, D - 1 + R - 1)

    for k in range(1, R):
        c = remote(feat_ref, panel.at[k], s_panel.at[k], r_panel.at[k], d, lax.rem(r + k, R))
        c.start()
        pending.append(c)

    def boundary(pack, recv, ss, rs):
        def one(k):
            dst = lax.rem(d + k, D)
            return remote(pack.at[pl.ds(at(dst, slots), slots)], recv.at[pl.ds(at(d, slots), slots)],
                          ss.at[k], rs.at[k], dst, r)

        def start():
            def body(k, carry):
                one(k).start()
                return carry
            lax.fori_loop(1, D, body, 0)
            mine = pl.ds(at(d, slots), slots)
            recv[mine, :] = pack[mine, :]

        def arrive():
            def body(k, carry):
                src = lax.rem(d + D - k, D)
                remote(pack.at[pl.ds(at(d, slots), slots)], recv.at[pl.ds(at(src, slots), slots)],
                       ss.at[k], rs.at[k], d, r).wait_recv()
                return carry
            lax.fori_loop(1, D, body, 0)

        def leave():
            def body(k, carry):
                one(k).wait_send()
                return carry
            lax.fori_loop(1, D, body, 0)

        return start, arrive, leave

    feat_start, feat_arrive, feat_leave = boundary(fpack, frecv, s_feat, r_feat)
    hist_start, hist_arrive, hist_leave = boundary(hpack, hrecv, s_hist, r_hist)
    back_start, back_arrive, back_leave = boundary(wpack, wrecv, s_back, r_back)
    feat_start()

    cotp[...] = jnp.zeros_like(cotp)
    cotp[0:C, :] = cot_ref[...]
    cot = split(cotp[...])
    for c in range(R):
        total = jnp.zeros((128, 128), F32)
        for k in range(tiles_ref.shape[0]):
            total = total + jnp.where(cols_ref[0, k] == c, tiles_ref[k], 0.0)
        adj[c] = total

    for k in range(1, R):
        dst = lax.rem(r + k, R)
        tsend[k] = dot(cot, split(adj[dst]))[:C8]
        c = remote(tsend.at[k], trecv.at[k], s_tr.at[k], r_tr.at[k], d, dst)
        c.start()
        pending.append(c)
    tsend[0] = dot(cot, split(adj[r]))[:C8]

    cw = cw_ref[...]
    wpack[...] = dot(split(cw.T), cot, NT)
    back_start()

    w2p[...] = jnp.zeros_like(w2p)
    w2p[0:C, :] = w2_ref[...]
    w2 = split(w2p[...])
    w2h[...] = w2[0]
    w2l[...] = w2[1]
    hist = split(hist_ref[...])
    hh[128:256, :] = hist[0]
    hl[128:256, :] = hist[1]
    hpack[...] = pick(send_pick, split(dot(hist, w2, NT)))
    hist_start()

    layer_in = dot(split(adj[r]), feat)
    for k in range(1, R):
        src = lax.rem(r + R - k, R)
        remote(feat_ref, panel.at[k], s_panel.at[k], r_panel.at[k], d, src).wait_recv()
        layer_in = layer_in + dot(split(adj[src]), split(panel[k]))
    cws = split(cw)
    feat_arrive()
    layer_in = layer_in + dot(cws, split(frecv[...]))
    pre = dot(split(layer_in), split(w1_ref[...]))
    sigma = jax.nn.sigmoid(pre)
    hid = split(pre * sigma)
    slope[...] = sigma * (1.0 + pre * (1.0 - sigma))
    hh[0:128, :] = hid[0]
    hl[0:128, :] = hid[1]
    proj[0] = dot((w2h[...], w2l[...]), (hh[0:128, :], hl[0:128, :]), NT)[:C8]
    for k in range(1, R):
        c = remote(proj.at[0], proj.at[k], s_proj.at[k], r_proj.at[k], d, lax.rem(r + k, R))
        c.start()
        pending.append(c)

    for k in range(1, R):
        remote(tsend.at[k], trecv.at[k], s_tr.at[k], r_tr.at[k], d, r).wait_recv()
    bg_t = tsend[0]
    for k in range(1, R):
        bg_t = bg_t + trecv[k]
    cotp[0:C8, :] = bg_t
    bg = split(cotp[...].T)
    back_arrive()
    hb_t = pick(back_pick, split(wrecv[...])).T[:C8]
    both = split(jnp.concatenate([bg_t, hb_t], axis=1))
    lit = split(layer_in.T)

    def block(lb):
        lanes = pl.ds(at(lb, 128), 128)
        base = at(lb, LB)
        gp = dot(bg, (w2h[:, lanes], w2l[:, lanes])) * slope[:, lanes]
        grads[pl.ds(base, F), :] = dot(lit, split(gp))
        grads[pl.ds(pl.multiple_of(base + F, 8), C8), :] = dot(both, (hh[:, lanes], hl[:, lanes]))
        if LB > F + C8:
            grads[pl.ds(pl.multiple_of(base + F + C8, 8), LB - F - C8), :] = jnp.zeros((LB - F - C8, 128), F32)

    def row_copy(k, j, dst):
        inner_block = lax.rem(i + 1 + j, nb)
        return remote(grads.at[pl.ds(at(dst * nb + inner_block, LB), LB)],
                      rb1.at[k, pl.ds(at(inner_block, LB), LB)],
                      s_row.at[k * nb + j], r_row.at[k * nb + j], d, dst)

    def others(step, carry):
        k = 1 + step // nb
        j = lax.rem(step, nb)
        dst = lax.rem(r + k, R)
        block(dst * nb + lax.rem(i + 1 + j, nb))
        row_copy(k, j, dst).start()
        return carry

    def mine(j, carry):
        block(r * nb + lax.rem(i + 1 + j, nb))
        return carry

    lax.fori_loop(0, (R - 1) * nb, others, 0)
    lax.fori_loop(0, nb, mine, 0)

    def inner_copy(k, t):
        dst = lax.rem(i + k, I)
        oo = lax.rem(o + 1 + t, O)
        return remote(a1.at[pl.ds(at(dst * O + oo, OP), OP)], rb2.at[k, pl.ds(at(oo, OP), OP)],
                      s_in.at[k * O + t], r_in.at[k * O + t], o * I + dst, r)

    def inner_send(k):
        for t in range(O):
            c = inner_copy(k, t)
            c.start()
            pending.append(c)

    for j in range(nb):
        inner_block = lax.rem(i + 1 + j, nb)
        rows = pl.ds(at(inner_block, LB), LB)
        total = grads[pl.ds(at(r * nb + inner_block, LB), LB), :]
        for k in range(1, R):
            row_copy(k, j, r).wait_recv()
            total = total + rb1[k, rows, :]
        a1[rows, :] = total
        if nb == I and j < nb - 1:
            inner_send(j + 1)
    if nb != I:
        for k in range(1, I):
            inner_send(k)

    hist_arrive()
    out = dot(cws, split(hrecv[...])).T[:C8]
    out = out + dot(split(proj[0]), split(adj[r]), NT)
    for k in range(1, R):
        src = lax.rem(r + R - k, R)
        remote(proj.at[0], proj.at[k], s_proj.at[k], r_proj.at[k], d, src).wait_recv()
        out = out + dot(split(proj[k]), split(adj[src]), NT)
    logits_ref[...] = out[:C]

    def spot(row, inner, outer):
        return pl.ds(at((row * I + inner) * O + outer, OP), OP)

    for t in range(O):
        oo = lax.rem(o + 1 + t, O)
        total = a1[pl.ds(at(i * O + oo, OP), OP), :]
        for k in range(1, I):
            inner_copy(k, t).wait_recv()
            total = total + rb2[k, pl.ds(at(oo, OP), OP), :]
        a2[t] = total
        if t < O - 1:
            c = remote(a2.at[t], rb3.at[t], s_out.at[t], r_out.at[t], oo * I + i, r)
            c.start()
            pending.append(c)
    total = a2[O - 1]
    for t in range(O - 1):
        remote(a2.at[t], rb3.at[t], s_out.at[t], r_out.at[t], d, r).wait_recv()
        total = total + rb3[t]
    full[spot(r, i, o), :] = total

    def gather(where, ss, rs, index, dom, row):
        return remote(full.at[where], full.at[where], ss.at[index], rs.at[index], dom, row)

    def launch(*rest):
        c = gather(*rest)
        c.start()
        pending.append(c)

    for k in range(1, O):
        launch(spot(r, i, o), s_gout, r_gout, k, lax.rem(o + k, O) * I + i, r)
    for kk in range(O):
        oo = lax.rem(o + O - kk, O)
        if kk:
            gather(spot(r, i, oo), s_gout, r_gout, kk, d, r).wait_recv()
        for k in range(1, I):
            launch(spot(r, i, oo), s_gin, r_gin, k * O + kk, o * I + lax.rem(i + k, I), r)

    def region(row, inner):
        return pl.ds(at(row * I + inner, IP), IP)

    for k in range(I):
        ii = lax.rem(i + I - k, I)
        if k:
            for kk in range(O):
                oo = lax.rem(o + O - kk, O)
                gather(spot(r, ii, oo), s_gin, r_gin, k * O + kk, d, r).wait_recv()
        for kr in range(1, R):
            launch(region(r, ii), s_grow, r_grow, kr * I + k, d, lax.rem(r + kr, R))
    for k in range(I):
        ii = lax.rem(i + I - k, I)
        for kr in range(1, R):
            src = lax.rem(r + R - kr, R)
            gather(region(src, ii), s_grow, r_grow, kr * I + k, d, r).wait_recv()

    for lb in range(NB):
        g1_ref[:, lb * 128:(lb + 1) * 128] = full[lb * LB:lb * LB + F, :]
        g2_ref[:, lb * 128:(lb + 1) * 128] = full[lb * LB + F:lb * LB + F + C, :]

    for c in pending:
        c.wait_send()

    def row_leave(step, carry):
        k = 1 + step // nb
        row_copy(k, lax.rem(step, nb), lax.rem(r + k, R)).wait_send()
        return carry

    lax.fori_loop(0, (R - 1) * nb, row_leave, 0)
    feat_leave()
    hist_leave()
    back_leave()


def on_device(D, R, features, history, tiles, tile_cols, cross_weight, send_rows, send_count, cotangent, w_one, w_two):
    O, I = factors(D)
    F = features.shape[1]
    H = w_one.shape[1]
    C = w_two.shape[1]
    slots = send_rows.shape[2]
    NS = D * slots
    C8 = round_up(C, 8)
    CP = round_up(C, 128)
    LB = round_up(F + C8, max(D * R, 8))
    NB = H // 128
    T = NB * LB
    TR = T // R
    IP = TR // I
    OP = IP // O
    V = pltpu.VMEM
    dma = pltpu.SemaphoreType.DMA
    scratch = [
        V((CP, 128), F32), V((CP, H), F32), V((CP, H), BF16), V((CP, H), BF16), V((R, 128, 128), F32),
        V((NS, F), F32), V((NS, F), F32), V((NS, CP), F32), V((NS, CP), F32), V((NS, CP), F32), V((NS, CP), F32),
        V((R, 128, F), F32), V((R, C8, 128), F32), V((R, C8, 128), F32), V((R, C8, 128), F32),
        V((256, H), BF16), V((256, H), BF16), V((128, H), F32),
        V((T, 128), F32), V((R, TR, 128), F32), V((TR, 128), F32), V((I, IP, 128), F32),
        V((O, OP, 128), F32), V((O, OP, 128), F32), V((T, 128), F32),
    ]
    for count in (D, D, D, R, R, R, NB, I * O, O, O, I * O, R * I):
        scratch += [dma((count,)), dma((count,))]
    in_vmem = pl.BlockSpec(memory_space=pltpu.VMEM)
    logits, grad_one, grad_two = pl.pallas_call(
        functools.partial(kernel, (D, R, O, I, LB)),
        out_shape=(
            jax.ShapeDtypeStruct((C, 128), F32),
            jax.ShapeDtypeStruct((F, H), F32),
            jax.ShapeDtypeStruct((C, H), F32),
        ),
        in_specs=[pl.BlockSpec(memory_space=pltpu.SMEM)] + [in_vmem] * 9,
        out_specs=(in_vmem, in_vmem, in_vmem),
        scratch_shapes=scratch,
        compiler_params=pltpu.CompilerParams(
            collective_id=0, has_side_effects=True, vmem_limit_bytes=60 * 1024 * 1024),
    )(tile_cols, features, history, tiles[0], cross_weight, send_rows[0].T, send_count, cotangent.T, w_one, w_two.T)
    return logits.T, grad_one, grad_two.T


def solution(mesh):
    both = ("dom", "row")
    placed = (
        P(both, None), P(both, None), P(both, None, None, None), P(both, None), P(both, None),
        P(both, None, None), P(both, None), P(both, None), P(), P(),
    )
    return jax.shard_map(
        functools.partial(on_device, mesh.shape["dom"], mesh.shape["row"]),
        mesh=mesh,
        in_specs=placed,
        out_specs=(P(both, None), P(), P()),
        check_vma=False,
    )
```

time: 194 us -> 51.4 us (0.26)
  waiting for transfers between devices: 131 us -> 0 us
  Pallas kernels: 0 us -> 46.2 us
  starting transfers between devices: 14.3 us -> 0 us
  between operations: 14.4 us -> 0.65 us
  matrix products: 11.4 us -> 0 us
  local copies, waits for them, and re-layouts: 12.1 us -> 4.35 us
  blocking collectives: 7.46 us -> 0 us
  other arithmetic: 2.67 us -> 0 us
    psum x1 -> x0, waiting for transfers between devices: 123 us -> none  [on_device(): grad_one, grad_two = lax.psum((grad_one, grad_two), ('dom', 'row'))]
    pallas_call x0 -> x1, Pallas kernels: none -> 46.2 us  [on_device(): pl.pallas_call(functools.partial(kernel, (D, R, O, I, LB)), out_shape=(ja...]
    all_to_all x2 -> x0, starting transfers between devices: 14.2 us -> none  [the longest x1 7.4 us: on_device(): lax.all_to_all(feat_out, 'dom', split_axis=0, concat_axis=0, tiled=True)]
    dot_general x13 -> x0, matrix products: 11.4 us -> none  [the longest x9 9.62 us: matmul(): jnp.dot(left, right, precision=HIGH, preferred_element_type=jnp.float32)]
    all_to_all x2 -> x0, waiting for transfers between devices: 7.7 us -> none  [the longest x1 7.7 us: on_device(): lax.all_to_all(hist_out, 'dom', split_axis=0, concat_axis=0, tiled=True)]
    all_gather x2 -> x0, blocking collectives: 7.46 us -> none  [the longest x1 4.97 us: on_device(): local_out = add_panel(lax.all_gather(projected, 'row', axis=0, tiled=True))]
    gather x6 -> x0, local copies, waits for them, and re-layouts: 5.24 us -> none  [the longest x4 2.92 us: add_panel(): picked = jnp.take(panel, jnp.clip(targets, 0, row_count - 1), axis=0)]
    unnamed x32 -> x5, local copies, waits for them, and re-layouts: 6.46 us -> 4.35 us
  transfers between devices with their start and end apart: 4 -> 0, of which waited for: 2 -> 0; matrix products, arithmetic and copies ran while one was open for 7% -> 0% of each run, Pallas kernels for 0% -> 0%
where the time goes in v1:
time: 51.4 us; the launch traced here: 51.2 us
  Pallas kernels  46.2 us (90%)
  local copies, waits for them, and re-layouts  4.35 us (8%)
  between operations  0.65 us (1%)
    pallas_call x1, Pallas kernels, on_device(): pl.pallas_call(functools.partial(kernel, (D, R, O, I, LB)), out_shape=(ja...  46.2 us
    unnamed x5, local copies, waits for them, and re-layouts  4.35 us

profile of v1, /device:TPU:1, one launch (start us, length us, event | category | flops | bytes accessed | tf_op | source)
XLA Modules:
  0.0 51.2 jit_solution(17222390377281725287)
XLA Ops:
  0.6 46.2 %shard_map.121 = (f32[172,128]{1,0:T(8,128)}, f32[128,1024]{1,0:T(8,128)}, f32[172,1024]{1,0:T(8,128)}) custom-call(s32[1,4]{1,0:T(1,128)} %cols_ref.1, f32[128,128]{1,0:T(8,128)} %feat_ref.1, f32[128,1024]{1,0:T(8,128)} %hist_ref.1, f32[4,128,128]{2,1,0:T(8,128)} %bitcast.10, f32[128,128]{1,0:T(8,128)} %cw_ref.1, s32[8,16]{1,0:T(8,128)} %bitcast.13, ...), custom_call_target="tpu_custom_call" | custom-call | tf_op jit(solution)/shard_map/pallas_call | solution.py:376
  46.8 0.0 copy-start
  46.8 1.6 %copy.16 = f32[128,172]{0,1:T(8,128)} copy(f32[128,172]{0,1:T(8,128)} %bitcast.12) | data formatting | bytes 176128
  48.4 1.9 %copy.17 = f32[128,1024]{1,0:T(8,128)} copy(f32[128,1024]{1,0:T(8,128)} %get-tuple-element.13) | data formatting | bytes 1048576
  50.3 0.0 copy-done
  50.3 0.9 %copy.18 = f32[1024,172]{0,1:T(8,128)} copy(f32[1024,172]{0,1:T(8,128)S(1)} %bitcast.8) | data formatting | bytes 1409024
Async XLA Ops:
  46.8 3.5 %copy-start = (f32[172,1024]{1,0:T(8,128)S(1)}, f32[172,1024]{1,0:T(8,128)}, u32[]{:S(2)}) copy-start(f32[172,1024]{1,0:T(8,128)} %get-tuple-element.8) | copy-start | bytes 2113540

commit v2 on v1

--- a/solution.py
+++ b/solution.py
@@ -42,13 +42,19 @@
 
 def kernel(
     sizes,
-    cols_ref, feat_ref, hist_ref, tiles_ref, cw_ref, rows_ref, count_ref, cot_ref, w1_ref, w2_ref,
+    cols_ref, *rest,
+):
+    sources, rest = rest[:9], rest[9:]
+    loaded, rest = rest[3:12], rest[:3] + rest[12:]
+    rows_ref, count_ref, feat_ref, tiles_ref, cot_ref, cw_ref, hist_ref, w2_ref, w1_ref = loaded
+    (
     logits_ref, g1_ref, g2_ref,
+    s_load,
     cotp, w2p, w2h, w2l, adj, fpack, frecv, hpack, hrecv, wpack, wrecv, panel,
     proj, tsend, trecv, hh, hl, slope, grads, rb1, a1, rb2, a2, rb3, full,
     s_feat, r_feat, s_hist, r_hist, s_back, r_back, s_panel, r_panel, s_proj, r_proj, s_tr, r_tr,
     s_row, r_row, s_in, r_in, s_out, r_out, s_gout, r_gout, s_gin, r_gin, s_grow, r_grow,
-):
+    ) = rest
     D, R, O, I, LB = sizes
     NB = w1_ref.shape[1] // 128
     nb = NB // R
@@ -84,7 +90,12 @@
 
     for k in range(1, R):
         pl.semaphore_signal(barrier, inc=1, device_id=(d, lax.rem(r + k, R)), device_id_type=MESH)
+    loads = [pltpu.make_async_copy(src, dst, s_load.at[n]) for n, (src, dst) in enumerate(zip(sources, loaded))]
+    for load in loads:
+        load.start()
     lax.fori_loop(1, D, greet, 0)
+    for load in loads[:3]:
+        load.wait()
 
     live = lax.broadcasted_iota(jnp.int32, (slots, D), 0) < count_ref[...]
     wanted = jnp.where(live, rows_ref[...], -1).astype(F32).astype(BF16)
@@ -102,13 +113,6 @@
     feat = split(feat_ref[...])
     fpack[...] = pick(send_pick, feat)
 
-    pl.semaphore_wait(barrier, D - 1 + R - 1)
-
-    for k in range(1, R):
-        c = remote(feat_ref, panel.at[k], s_panel.at[k], r_panel.at[k], d, lax.rem(r + k, R))
-        c.start()
-        pending.append(c)
-
     def boundary(pack, recv, ss, rs):
         def one(k):
             dst = lax.rem(d + k, D)
@@ -142,8 +146,8 @@
     feat_start, feat_arrive, feat_leave = boundary(fpack, frecv, s_feat, r_feat)
     hist_start, hist_arrive, hist_leave = boundary(hpack, hrecv, s_hist, r_hist)
     back_start, back_arrive, back_leave = boundary(wpack, wrecv, s_back, r_back)
-    feat_start()
-
+    for load in loads[3:]:
+        load.wait()
     cotp[...] = jnp.zeros_like(cotp)
     cotp[0:C, :] = cot_ref[...]
     cot = split(cotp[...])
@@ -156,14 +160,10 @@
     for k in range(1, R):
         dst = lax.rem(r + k, R)
         tsend[k] = dot(cot, split(adj[dst]))[:C8]
-        c = remote(tsend.at[k], trecv.at[k], s_tr.at[k], r_tr.at[k], d, dst)
-        c.start()
-        pending.append(c)
     tsend[0] = dot(cot, split(adj[r]))[:C8]
 
     cw = cw_ref[...]
     wpack[...] = dot(split(cw.T), cot, NT)
-    back_start()
 
     w2p[...] = jnp.zeros_like(w2p)
     w2p[0:C, :] = w2_ref[...]
@@ -174,9 +174,22 @@
     hh[128:256, :] = hist[0]
     hl[128:256, :] = hist[1]
     hpack[...] = pick(send_pick, split(dot(hist, w2, NT)))
+
+    pl.semaphore_wait(barrier, D - 1 + R - 1)
+
+    for k in range(1, R):
+        c = remote(feat_ref, panel.at[k], s_panel.at[k], r_panel.at[k], d, lax.rem(r + k, R))
+        c.start()
+        pending.append(c)
+    feat_start()
+    for k in range(1, R):
+        c = remote(tsend.at[k], trecv.at[k], s_tr.at[k], r_tr.at[k], d, lax.rem(r + k, R))
+        c.start()
+        pending.append(c)
+    back_start()
     hist_start()
-
     layer_in = dot(split(adj[r]), feat)
+
     for k in range(1, R):
         src = lax.rem(r + R - k, R)
         remote(feat_ref, panel.at[k], s_panel.at[k], r_panel.at[k], d, src).wait_recv()
@@ -217,52 +230,78 @@
         if LB > F + C8:
             grads[pl.ds(pl.multiple_of(base + F + C8, 8), LB - F - C8), :] = jnp.zeros((LB - F - C8, 128), F32)
 
+    bits = I.bit_length() - 1
+
+    def low(e):
+        return (e & -e).bit_length() - 1 if e else bits
+
+    order = [e for step in range(bits) for e in sorted(
+        (e for e in range(1, I) if low(e) == step), key=lambda e: (low(e & (e - 1)), e))] + [0]
+
+    def flipped(row, e):
+        place = i
+        for step in range(bits):
+            if e >> step & 1:
+                mask = 0
+                for bit in range(bits):
+                    mask = mask + jnp.where(lax.rem(row + step, bits) == bit, 1 << bit, 0)
+                place = place + mask * (1 - 2 * lax.rem(i // mask, 2))
+        return place
+
+    def lane_block(row, j):
+        return flipped(row, order[j]) if nb == I else j
+
     def row_copy(k, j, dst):
-        inner_block = lax.rem(i + 1 + j, nb)
-        return remote(grads.at[pl.ds(at(dst * nb + inner_block, LB), LB)],
-                      rb1.at[k, pl.ds(at(inner_block, LB), LB)],
+        where = lane_block(dst, j)
+        return remote(grads.at[pl.ds(at(dst * nb + where, LB), LB)],
+                      rb1.at[k, pl.ds(at(where, LB), LB)],
                       s_row.at[k * nb + j], r_row.at[k * nb + j], d, dst)
 
-    def others(step, carry):
-        k = 1 + step // nb
-        j = lax.rem(step, nb)
-        dst = lax.rem(r + k, R)
-        block(dst * nb + lax.rem(i + 1 + j, nb))
-        row_copy(k, j, dst).start()
-        return carry
-
-    def mine(j, carry):
-        block(r * nb + lax.rem(i + 1 + j, nb))
-        return carry
-
-    lax.fori_loop(0, (R - 1) * nb, others, 0)
-    lax.fori_loop(0, nb, mine, 0)
-
-    def inner_copy(k, t):
-        dst = lax.rem(i + k, I)
+    partner = [o * I + flipped(r, 1 << step) for step in range(bits)]
+    home = [flipped(r, e) for e in range(I)]
+
+    def sum_piece(e, t):
         oo = lax.rem(o + 1 + t, O)
-        return remote(a1.at[pl.ds(at(dst * O + oo, OP), OP)], rb2.at[k, pl.ds(at(oo, OP), OP)],
-                      s_in.at[k * O + t], r_in.at[k * O + t], o * I + dst, r)
-
-    def inner_send(k):
+        total = a1[pl.ds(at(home[e] * O + oo, OP), OP), :]
+        for step in range(low(e)):
+            slot = e | 1 << step
+            remote(a2.at[t], rb2.at[slot, pl.ds(at(oo, OP), OP)], s_in.at[slot * O + t], r_in.at[slot * O + t],
+                   d, r).wait_recv()
+            total = total + rb2[slot, pl.ds(at(oo, OP), OP), :]
+        return total
+
+    def pass_on(e):
         for t in range(O):
-            c = inner_copy(k, t)
+            oo = lax.rem(o + 1 + t, O)
+            piece = pl.ds(at(home[e] * O + oo, OP), OP)
+            if low(e):
+                a1[piece, :] = sum_piece(e, t)
+            c = remote(a1.at[piece], rb2.at[e, pl.ds(at(oo, OP), OP)], s_in.at[e * O + t], r_in.at[e * O + t],
+                       partner[low(e)], r)
             c.start()
             pending.append(c)
 
+    for k in range(1, R):
+        dst = lax.rem(r + k, R)
+        for j in range(nb):
+            block(dst * nb + lane_block(dst, j))
+            c = row_copy(k, j, dst)
+            c.start()
+            pending.append(c)
     for j in range(nb):
-        inner_block = lax.rem(i + 1 + j, nb)
-        rows = pl.ds(at(inner_block, LB), LB)
-        total = grads[pl.ds(at(r * nb + inner_block, LB), LB), :]
+        where = lane_block(r, j)
+        block(r * nb + where)
+        rows = pl.ds(at(where, LB), LB)
+        total = grads[pl.ds(at(r * nb + where, LB), LB), :]
         for k in range(1, R):
             row_copy(k, j, r).wait_recv()
             total = total + rb1[k, rows, :]
         a1[rows, :] = total
-        if nb == I and j < nb - 1:
-            inner_send(j + 1)
-    if nb != I:
-        for k in range(1, I):
-            inner_send(k)
+        if nb == I and low(order[j]) == 0:
+            pass_on(order[j])
+    for e in order[:-1]:
+        if nb != I or low(e):
+            pass_on(e)
 
     hist_arrive()
     out = dot(cws, split(hrecv[...])).T[:C8]
@@ -278,11 +317,7 @@
 
     for t in range(O):
         oo = lax.rem(o + 1 + t, O)
-        total = a1[pl.ds(at(i * O + oo, OP), OP), :]
-        for k in range(1, I):
-            inner_copy(k, t).wait_recv()
-            total = total + rb2[k, pl.ds(at(oo, OP), OP), :]
-        a2[t] = total
+        a2[t] = sum_piece(0, t)
         if t < O - 1:
             c = remote(a2.at[t], rb3.at[t], s_out.at[t], r_out.at[t], oo * I + i, r)
             c.start()
@@ -303,29 +338,31 @@
 
     for k in range(1, O):
         launch(spot(r, i, o), s_gout, r_gout, k, lax.rem(o + k, O) * I + i, r)
-    for kk in range(O):
-        oo = lax.rem(o + O - kk, O)
-        if kk:
-            gather(spot(r, i, oo), s_gout, r_gout, kk, d, r).wait_recv()
-        for k in range(1, I):
-            launch(spot(r, i, oo), s_gin, r_gin, k * O + kk, o * I + lax.rem(i + k, I), r)
 
     def region(row, inner):
         return pl.ds(at(row * I + inner, IP), IP)
 
-    for k in range(I):
-        ii = lax.rem(i + I - k, I)
-        if k:
-            for kk in range(O):
-                oo = lax.rem(o + O - kk, O)
-                gather(spot(r, ii, oo), s_gin, r_gin, k * O + kk, d, r).wait_recv()
-        for kr in range(1, R):
-            launch(region(r, ii), s_grow, r_grow, kr * I + k, d, lax.rem(r + kr, R))
-    for k in range(I):
-        ii = lax.rem(i + I - k, I)
+    def handle(e, kk):
+        oo = lax.rem(o + O - kk, O)
+        if e:
+            gather(spot(r, home[e], oo), s_gin, r_gin, e * O + kk, d, r).wait_recv()
+        elif kk:
+            gather(spot(r, i, oo), s_gout, r_gout, kk, d, r).wait_recv()
+        for step in reversed(range(low(e))):
+            launch(spot(r, home[e], oo), s_gin, r_gin, (e | 1 << step) * O + kk, partner[step], r)
+        if kk == O - 1:
+            for kr in range(1, R):
+                launch(region(r, home[e]), s_grow, r_grow, kr * I + e, d, lax.rem(r + kr, R))
+
+    ranked = sorted(range(I), key=lambda e: (e.bit_count(), e))
+    for turn in range(O + bits):
+        for e in ranked:
+            if 0 <= turn - e.bit_count() < O:
+                handle(e, turn - e.bit_count())
+    for e in ranked:
         for kr in range(1, R):
             src = lax.rem(r + R - kr, R)
-            gather(region(src, ii), s_grow, r_grow, kr * I + k, d, r).wait_recv()
+            gather(region(src, flipped(src, e)), s_grow, r_grow, kr * I + e, d, r).wait_recv()
 
     for lb in range(NB):
         g1_ref[:, lb * 128:(lb + 1) * 128] = full[lb * LB:lb * LB + F, :]
@@ -334,12 +371,6 @@
     for c in pending:
         c.wait_send()
 
-    def row_leave(step, carry):
-        k = 1 + step // nb
-        row_copy(k, lax.rem(step, nb), lax.rem(r + k, R)).wait_send()
-        return carry
-
-    lax.fori_loop(0, (R - 1) * nb, row_leave, 0)
     feat_leave()
     hist_leave()
     back_leave()
@@ -373,6 +404,8 @@
     for count in (D, D, D, R, R, R, NB, I * O, O, O, I * O, R * I):
         scratch += [dma((count,)), dma((count,))]
     in_vmem = pl.BlockSpec(memory_space=pltpu.VMEM)
+    operands = (send_rows[0].T, send_count, features, tiles[0], cotangent.T, cross_weight, history, w_two.T, w_one)
+    scratch = [V(x.shape, x.dtype) for x in operands] + [dma((len(operands),))] + scratch
     logits, grad_one, grad_two = pl.pallas_call(
         functools.partial(kernel, (D, R, O, I, LB)),
         out_shape=(
@@ -380,12 +413,12 @@
             jax.ShapeDtypeStruct((F, H), F32),
             jax.ShapeDtypeStruct((C, H), F32),
         ),
-        in_specs=[pl.BlockSpec(memory_space=pltpu.SMEM)] + [in_vmem] * 9,
+        in_specs=[pl.BlockSpec(memory_space=pltpu.SMEM)] + [pl.BlockSpec(memory_space=pl.ANY)] * len(operands),
         out_specs=(in_vmem, in_vmem, in_vmem),
         scratch_shapes=scratch,
         compiler_params=pltpu.CompilerParams(
             collective_id=0, has_side_effects=True, vmem_limit_bytes=60 * 1024 * 1024),
-    )(tile_cols, features, history, tiles[0], cross_weight, send_rows[0].T, send_count, cotangent.T, w_one, w_two.T)
+    )(tile_cols, *operands)
     return logits.T, grad_one, grad_two.T
 
 

time: 51.4 us -> 53 us (1.031)
  Pallas kernels: 46.2 us -> 47.8 us
    pallas_call x1, Pallas kernels: 46.2 us -> 47.8 us  [on_device(): pl.pallas_call(functools.partial(kernel, (D, R, O, I, LB)), out_shape=(ja...]
where the time goes in v2:
time: 53 us; the launch traced here: 52.8 us
  Pallas kernels  47.8 us (90%)
  local copies, waits for them, and re-layouts  4.35 us (8%)
  between operations  0.65 us (1%)
    pallas_call x1, Pallas kernels, on_device(): pl.pallas_call(functools.partial(kernel, (D, R, O, I, LB)), out_shape=(ja...  47.8 us
    unnamed x5, local copies, waits for them, and re-layouts  4.35 us

profile of v2, /device:TPU:1, one launch (start us, length us, event | category | flops | bytes accessed | tf_op | source)
XLA Modules:
  0.0 52.8 jit_solution(8684726919851158481)
XLA Ops:
  0.6 47.8 %shard_map.121 = (f32[172,128]{1,0:T(8,128)}, f32[128,1024]{1,0:T(8,128)}, f32[172,1024]{1,0:T(8,128)}) custom-call(s32[1,4]{1,0:T(1,128)} %cols_ref.1, s32[8,16]{1,0:T(8,128)} %bitcast.13, s32[1,16]{1,0:T(1,128)} %rest_1_.1, f32[128,128]{1,0:T(8,128)} %rest_2_.1, f32[4,128,128]{2,1,0:T(8,128)} %bitcast.10, f32[172,128]{1,0:T(8,128)} %bitcast.11, ...), custom_call_target="tpu_custom_call" | custom-call | tf_op jit(solution)/shard_map/pallas_call | solution.py:409
  48.4 0.0 copy-start
  48.5 1.6 %copy.16 = f32[128,172]{0,1:T(8,128)} copy(f32[128,172]{0,1:T(8,128)} %bitcast.12) | data formatting | bytes 176128
  50.1 1.9 %copy.17 = f32[128,1024]{1,0:T(8,128)} copy(f32[128,1024]{1,0:T(8,128)} %get-tuple-element.13) | data formatting | bytes 1048576
  51.9 0.0 copy-done
  51.9 0.9 %copy.18 = f32[1024,172]{0,1:T(8,128)} copy(f32[1024,172]{0,1:T(8,128)S(1)} %bitcast.8) | data formatting | bytes 1409024
Async XLA Ops:
  48.4 3.5 %copy-start = (f32[172,1024]{1,0:T(8,128)S(1)}, f32[172,1024]{1,0:T(8,128)}, u32[]{:S(2)}) copy-start(f32[172,1024]{1,0:T(8,128)} %get-tuple-element.8) | copy-start | bytes 2113540

commit v3 on v1

--- a/solution.py
+++ b/solution.py
@@ -42,13 +42,19 @@
 
 def kernel(
     sizes,
-    cols_ref, feat_ref, hist_ref, tiles_ref, cw_ref, rows_ref, count_ref, cot_ref, w1_ref, w2_ref,
+    cols_ref, *rest,
+):
+    sources, rest = rest[:9], rest[9:]
+    loaded, rest = rest[3:12], rest[:3] + rest[12:]
+    rows_ref, count_ref, feat_ref, tiles_ref, cot_ref, cw_ref, hist_ref, w2_ref, w1_ref = loaded
+    (
     logits_ref, g1_ref, g2_ref,
+    s_load,
     cotp, w2p, w2h, w2l, adj, fpack, frecv, hpack, hrecv, wpack, wrecv, panel,
     proj, tsend, trecv, hh, hl, slope, grads, rb1, a1, rb2, a2, rb3, full,
     s_feat, r_feat, s_hist, r_hist, s_back, r_back, s_panel, r_panel, s_proj, r_proj, s_tr, r_tr,
     s_row, r_row, s_in, r_in, s_out, r_out, s_gout, r_gout, s_gin, r_gin, s_grow, r_grow,
-):
+    ) = rest
     D, R, O, I, LB = sizes
     NB = w1_ref.shape[1] // 128
     nb = NB // R
@@ -84,7 +90,12 @@
 
     for k in range(1, R):
         pl.semaphore_signal(barrier, inc=1, device_id=(d, lax.rem(r + k, R)), device_id_type=MESH)
+    loads = [pltpu.make_async_copy(src, dst, s_load.at[n]) for n, (src, dst) in enumerate(zip(sources, loaded))]
+    for load in loads:
+        load.start()
     lax.fori_loop(1, D, greet, 0)
+    for load in loads[:3]:
+        load.wait()
 
     live = lax.broadcasted_iota(jnp.int32, (slots, D), 0) < count_ref[...]
     wanted = jnp.where(live, rows_ref[...], -1).astype(F32).astype(BF16)
@@ -102,13 +113,6 @@
     feat = split(feat_ref[...])
     fpack[...] = pick(send_pick, feat)
 
-    pl.semaphore_wait(barrier, D - 1 + R - 1)
-
-    for k in range(1, R):
-        c = remote(feat_ref, panel.at[k], s_panel.at[k], r_panel.at[k], d, lax.rem(r + k, R))
-        c.start()
-        pending.append(c)
-
     def boundary(pack, recv, ss, rs):
         def one(k):
             dst = lax.rem(d + k, D)
@@ -142,8 +146,8 @@
     feat_start, feat_arrive, feat_leave = boundary(fpack, frecv, s_feat, r_feat)
     hist_start, hist_arrive, hist_leave = boundary(hpack, hrecv, s_hist, r_hist)
     back_start, back_arrive, back_leave = boundary(wpack, wrecv, s_back, r_back)
-    feat_start()
-
+    for load in loads[3:]:
+        load.wait()
     cotp[...] = jnp.zeros_like(cotp)
     cotp[0:C, :] = cot_ref[...]
     cot = split(cotp[...])
@@ -156,14 +160,10 @@
     for k in range(1, R):
         dst = lax.rem(r + k, R)
         tsend[k] = dot(cot, split(adj[dst]))[:C8]
-        c = remote(tsend.at[k], trecv.at[k], s_tr.at[k], r_tr.at[k], d, dst)
-        c.start()
-        pending.append(c)
     tsend[0] = dot(cot, split(adj[r]))[:C8]
 
     cw = cw_ref[...]
     wpack[...] = dot(split(cw.T), cot, NT)
-    back_start()
 
     w2p[...] = jnp.zeros_like(w2p)
     w2p[0:C, :] = w2_ref[...]
@@ -174,15 +174,27 @@
     hh[128:256, :] = hist[0]
     hl[128:256, :] = hist[1]
     hpack[...] = pick(send_pick, split(dot(hist, w2, NT)))
-    hist_start()
-
+
+    pl.semaphore_wait(barrier, D - 1 + R - 1)
+
+    for k in range(1, R):
+        c = remote(feat_ref, panel.at[k], s_panel.at[k], r_panel.at[k], d, lax.rem(r + k, R))
+        c.start()
+        pending.append(c)
+    feat_start()
+    for k in range(1, R):
+        c = remote(tsend.at[k], trecv.at[k], s_tr.at[k], r_tr.at[k], d, lax.rem(r + k, R))
+        c.start()
+        pending.append(c)
     layer_in = dot(split(adj[r]), feat)
+
     for k in range(1, R):
         src = lax.rem(r + R - k, R)
         remote(feat_ref, panel.at[k], s_panel.at[k], r_panel.at[k], d, src).wait_recv()
         layer_in = layer_in + dot(split(adj[src]), split(panel[k]))
     cws = split(cw)
     feat_arrive()
+    back_start()
     layer_in = layer_in + dot(cws, split(frecv[...]))
     pre = dot(split(layer_in), split(w1_ref[...]))
     sigma = jax.nn.sigmoid(pre)
@@ -196,6 +208,8 @@
         c.start()
         pending.append(c)
 
+    hist_start()
+
     for k in range(1, R):
         remote(tsend.at[k], trecv.at[k], s_tr.at[k], r_tr.at[k], d, r).wait_recv()
     bg_t = tsend[0]
@@ -244,12 +258,6 @@
         return remote(a1.at[pl.ds(at(dst * O + oo, OP), OP)], rb2.at[k, pl.ds(at(oo, OP), OP)],
                       s_in.at[k * O + t], r_in.at[k * O + t], o * I + dst, r)
 
-    def inner_send(k):
-        for t in range(O):
-            c = inner_copy(k, t)
-            c.start()
-            pending.append(c)
-
     for j in range(nb):
         inner_block = lax.rem(i + 1 + j, nb)
         rows = pl.ds(at(inner_block, LB), LB)
@@ -258,11 +266,11 @@
             row_copy(k, j, r).wait_recv()
             total = total + rb1[k, rows, :]
         a1[rows, :] = total
-        if nb == I and j < nb - 1:
-            inner_send(j + 1)
-    if nb != I:
+    for t in range(O):
         for k in range(1, I):
-            inner_send(k)
+            c = inner_copy(k, t)
+            c.start()
+            pending.append(c)
 
     hist_arrive()
     out = dot(cws, split(hrecv[...])).T[:C8]
@@ -343,6 +351,20 @@
     feat_leave()
     hist_leave()
     back_leave()
+
+
+def hand_over(*refs):
+    given, out, held = refs[0:3], refs[3:6], refs[6:9]
+    s_get, s_put = refs[9:]
+    gets = [pltpu.make_async_copy(given[n], held[n], s_get.at[n]) for n in range(3)]
+    puts = [pltpu.make_async_copy(held[n], out[n], s_put.at[n]) for n in range(3)]
+    for get in gets:
+        get.start()
+    for get, put in zip(gets, puts):
+        get.wait()
+        put.start()
+    for put in puts:
+        put.wait()
 
 
 def on_device(D, R, features, history, tiles, tile_cols, cross_weight, send_rows, send_count, cotangent, w_one, w_two):
@@ -373,6 +395,8 @@
     for count in (D, D, D, R, R, R, NB, I * O, O, O, I * O, R * I):
         scratch += [dma((count,)), dma((count,))]
     in_vmem = pl.BlockSpec(memory_space=pltpu.VMEM)
+    operands = (send_rows[0].T, send_count, features, tiles[0], cotangent.T, cross_weight, history, w_two.T, w_one)
+    scratch = [V(x.shape, x.dtype) for x in operands] + [dma((len(operands),))] + scratch
     logits, grad_one, grad_two = pl.pallas_call(
         functools.partial(kernel, (D, R, O, I, LB)),
         out_shape=(
@@ -380,12 +404,21 @@
             jax.ShapeDtypeStruct((F, H), F32),
             jax.ShapeDtypeStruct((C, H), F32),
         ),
-        in_specs=[pl.BlockSpec(memory_space=pltpu.SMEM)] + [in_vmem] * 9,
+        in_specs=[pl.BlockSpec(memory_space=pltpu.SMEM)] + [pl.BlockSpec(memory_space=pl.ANY)] * len(operands),
         out_specs=(in_vmem, in_vmem, in_vmem),
         scratch_shapes=scratch,
         compiler_params=pltpu.CompilerParams(
             collective_id=0, has_side_effects=True, vmem_limit_bytes=60 * 1024 * 1024),
-    )(tile_cols, features, history, tiles[0], cross_weight, send_rows[0].T, send_count, cotangent.T, w_one, w_two.T)
+    )(tile_cols, *operands)
+    results = (logits, grad_one, grad_two)
+    anywhere = [pl.BlockSpec(memory_space=pl.ANY)] * 3
+    logits, grad_one, grad_two = pl.pallas_call(
+        hand_over,
+        out_shape=tuple(jax.ShapeDtypeStruct(x.shape, x.dtype) for x in results),
+        in_specs=anywhere,
+        out_specs=tuple(anywhere),
+        scratch_shapes=[V(x.shape, x.dtype) for x in results] + [dma((3,)), dma((3,))],
+    )(*results)
     return logits.T, grad_one, grad_two.T
 
 

time: 51.4 us -> 50.4 us (0.981)
  local copies, waits for them, and re-layouts: 4.35 us -> 0 us
  Pallas kernels: 46.2 us -> 49.6 us
    unnamed x5 -> x0, local copies, waits for them, and re-layouts: 4.35 us -> none
    pallas_call x0 -> x1, Pallas kernels: none -> 2.23 us  [on_device(): pl.pallas_call(hand_over, out_shape=tuple((jax.ShapeDtypeStruct(x.shape,...]
    pallas_call x1, Pallas kernels: 46.2 us -> 47.3 us  [on_device(): pl.pallas_call(functools.partial(kernel, (D, R, O, I, LB)), out_shape=(ja...]
where the time goes in v3:
time: 50.4 us; the launch traced here: 50.2 us
  Pallas kernels  49.6 us (98%)
  between operations  0.64 us (1%)
    pallas_call x1, Pallas kernels, on_device(): pl.pallas_call(functools.partial(kernel, (D, R, O, I, LB)), out_shape=(ja...  47.3 us
    pallas_call x1, Pallas kernels, on_device(): pl.pallas_call(hand_over, out_shape=tuple((jax.ShapeDtypeStruct(x.shape,...  2.23 us

profile of v3, /device:TPU:1, one launch (start us, length us, event | category | flops | bytes accessed | tf_op | source)
XLA Modules:
  0.0 50.2 jit_solution(5075612948644748763)
XLA Ops:
  0.6 47.3 %shard_map.121 = (f32[172,128]{1,0:T(8,128)}, f32[128,1024]{1,0:T(8,128)}, f32[172,1024]{1,0:T(8,128)}) custom-call(s32[1,4]{1,0:T(1,128)} %cols_ref.1, s32[8,16]{1,0:T(8,128)} %bitcast.11, s32[1,16]{1,0:T(1,128)} %rest_1_.1, f32[128,128]{1,0:T(8,128)} %rest_2_.1, f32[4,128,128]{2,1,0:T(8,128)} %bitcast.9, f32[172,128]{1,0:T(8,128)} %bitcast.10, ...), custom_call_target="tpu_custom_call" | custom-call | tf_op jit(solution)/shard_map/pallas_call | solution.py:400
  48.0 2.2 %shard_map.122 = (f32[172,128]{1,0:T(8,128)}, f32[128,1024]{1,0:T(8,128)}, f32[172,1024]{1,0:T(8,128)}) custom-call(f32[172,128]{1,0:T(8,128)} %get-tuple-element.9.refs_0_, f32[128,1024]{1,0:T(8,128)} %get-tuple-element.10.refs_1_, f32[172,1024]{1,0:T(8,128)} %get-tuple-element.11.refs_2_), custom_call_target="tpu_custom_call" | custom-call | tf_op jit(solution)/shard_map/pallas_call | solution.py:415

commit v4 on v3

--- a/solution.py
+++ b/solution.py
@@ -146,6 +146,14 @@
     feat_start, feat_arrive, feat_leave = boundary(fpack, frecv, s_feat, r_feat)
     hist_start, hist_arrive, hist_leave = boundary(hpack, hrecv, s_hist, r_hist)
     back_start, back_arrive, back_leave = boundary(wpack, wrecv, s_back, r_back)
+    pl.semaphore_wait(barrier, D - 1 + R - 1)
+
+    for k in range(1, R):
+        c = remote(feat_ref, panel.at[k], s_panel.at[k], r_panel.at[k], d, lax.rem(r + k, R))
+        c.start()
+        pending.append(c)
+    feat_start()
+
     for load in loads[3:]:
         load.wait()
     cotp[...] = jnp.zeros_like(cotp)
@@ -160,10 +168,14 @@
     for k in range(1, R):
         dst = lax.rem(r + k, R)
         tsend[k] = dot(cot, split(adj[dst]))[:C8]
+        c = remote(tsend.at[k], trecv.at[k], s_tr.at[k], r_tr.at[k], d, dst)
+        c.start()
+        pending.append(c)
     tsend[0] = dot(cot, split(adj[r]))[:C8]
 
     cw = cw_ref[...]
     wpack[...] = dot(split(cw.T), cot, NT)
+    back_start()
 
     w2p[...] = jnp.zeros_like(w2p)
     w2p[0:C, :] = w2_ref[...]
@@ -175,17 +187,6 @@
     hl[128:256, :] = hist[1]
     hpack[...] = pick(send_pick, split(dot(hist, w2, NT)))
 
-    pl.semaphore_wait(barrier, D - 1 + R - 1)
-
-    for k in range(1, R):
-        c = remote(feat_ref, panel.at[k], s_panel.at[k], r_panel.at[k], d, lax.rem(r + k, R))
-        c.start()
-        pending.append(c)
-    feat_start()
-    for k in range(1, R):
-        c = remote(tsend.at[k], trecv.at[k], s_tr.at[k], r_tr.at[k], d, lax.rem(r + k, R))
-        c.start()
-        pending.append(c)
     layer_in = dot(split(adj[r]), feat)
 
     for k in range(1, R):
@@ -194,7 +195,6 @@
         layer_in = layer_in + dot(split(adj[src]), split(panel[k]))
     cws = split(cw)
     feat_arrive()
-    back_start()
     layer_in = layer_in + dot(cws, split(frecv[...]))
     pre = dot(split(layer_in), split(w1_ref[...]))
     sigma = jax.nn.sigmoid(pre)

time: 50.4 us -> 46.3 us (0.919)
  Pallas kernels: 49.6 us -> 45.5 us
    pallas_call x1, Pallas kernels: 47.3 us -> 43.3 us  [on_device(): pl.pallas_call(functools.partial(kernel, (D, R, O, I, LB)), out_shape=(ja...]
where the time goes in v4:
time: 46.3 us; the launch traced here: 46.1 us
  Pallas kernels  45.5 us (98%)
  between operations  0.64 us (1%)
    pallas_call x1, Pallas kernels, on_device(): pl.pallas_call(functools.partial(kernel, (D, R, O, I, LB)), out_shape=(ja...  43.3 us
    pallas_call x1, Pallas kernels, on_device(): pl.pallas_call(hand_over, out_shape=tuple((jax.ShapeDtypeStruct(x.shape,...  2.23 us

profile of v4, /device:TPU:1, one launch (start us, length us, event | category | flops | bytes accessed | tf_op | source)
XLA Modules:
  0.0 46.1 jit_solution(9927629815675588655)
XLA Ops:
  0.6 43.3 %shard_map.121 = (f32[172,128]{1,0:T(8,128)}, f32[128,1024]{1,0:T(8,128)}, f32[172,1024]{1,0:T(8,128)}) custom-call(s32[1,4]{1,0:T(1,128)} %cols_ref.1, s32[8,16]{1,0:T(8,128)} %bitcast.11, s32[1,16]{1,0:T(1,128)} %rest_1_.1, f32[128,128]{1,0:T(8,128)} %rest_2_.1, f32[4,128,128]{2,1,0:T(8,128)} %bitcast.9, f32[172,128]{1,0:T(8,128)} %bitcast.10, ...), custom_call_target="tpu_custom_call" | custom-call | tf_op jit(solution)/shard_map/pallas_call | solution.py:400
  43.9 2.2 %shard_map.122 = (f32[172,128]{1,0:T(8,128)}, f32[128,1024]{1,0:T(8,128)}, f32[172,1024]{1,0:T(8,128)}) custom-call(f32[172,128]{1,0:T(8,128)} %get-tuple-element.9.refs_0_, f32[128,1024]{1,0:T(8,128)} %get-tuple-element.10.refs_1_, f32[172,1024]{1,0:T(8,128)} %get-tuple-element.11.refs_2_), custom_call_target="tpu_custom_call" | custom-call | tf_op jit(solution)/shard_map/pallas_call | solution.py:415
